TPU v7x, 256 devices: a whole 4x4x8 slice. The times are simulated.
256 devices in a mesh: row: 16 (over y, z_lo), col: 16 (over x, z_hi, core).
Axes of the slice: x: 4, y: 4, z: 8 (z_hi: 2, z_lo: 4; z = z_hi * 4 + z_lo), core: 2. Of those that a mesh axis runs over, the one named last changes fastest.
Arguments:
- features: float32 [65536, 128], P(('col', 'row')), may hold values from -6 to 6
- weight: float32 [128, 128], replicated, may hold values from -4 to 4
- bias_vector: float32 [128], replicated, may hold values from -4 to 4
- out_grad: float32 [65536, 128], P(('row', 'col')), may hold values from -6 to 6
- adj_tiles: int32 [16, 16, 128, 128, 128], P('row', 'col'), may hold values 0 or 1
- tile_slots: int32 [16, 16, 128], P('row', 'col'), may hold values from 0 to 1023, as said below
- tile_counts: int32 [16, 16], P('row', 'col'), may hold values from 17 to 128, as said below
Outputs:
- activated: float32 [65536, 128], P(('row', 'col'))
- feature_grad: float32 [65536, 128], P(('col', 'row'))
- weight_grad: float32 [128, 128], replicated
- bias_grad: float32 [128], replicated
Inputs may be any that keep to these rules, and one draw needn't show every extreme that they name: `tile_slots`: each block's slots name distinct positions r * 32 + c of its 32 x 32 tiles. Some block is full in every draw; slots from tile_counts on are ignored.
All inputs are finite; a program needn't handle non-finite values. No bound on the sum of `adj_tiles` on one device may be relied on, other than what follows from the above.
Results may differ from a plain program's by a relative error of at most 0.0003.
Values sent between devices are 32-bit elements; how exact they have to be, the bound alone decides.
A program may use at most 128 MiB of HBM per device.

v0:
```python
import jax
import jax.numpy as jnp
from jax import lax
from jax.sharding import PartitionSpec as P

TILE = 128


def dense_step(aggregated, weight, bias_vector, cotangent):
    preact = jnp.dot(aggregated, weight, precision=lax.Precision.HIGHEST) + bias_vector
    logistic = jax.nn.sigmoid(preact)
    activated = preact * logistic
    pre_grad = cotangent * logistic * (1.0 + preact * (1.0 - logistic))
    weight_part = jnp.dot(aggregated.T, pre_grad, precision=lax.Precision.HIGHEST)
    bias_part = jnp.sum(pre_grad, axis=0)
    back_rows = jnp.dot(pre_grad, weight.T, precision=lax.Precision.HIGHEST)
    return (activated, weight_part, bias_part, back_rows)


def local(features, weight, bias_vector, out_grad, adj_tiles, tile_slots, tile_counts):
    row_count = lax.axis_size("row")
    col_count = lax.axis_size("col")
    node_rows = features.shape[0]
    width = features.shape[1]
    tile_rows = node_rows * col_count // TILE
    tile_cols = node_rows * row_count // TILE
    adjacency = adj_tiles[0, 0].astype(jnp.float32)
    slots = tile_slots[0, 0]
    slot_total = slots.shape[0]
    live_mask = (jnp.arange(slot_total) < tile_counts[0, 0]).astype(jnp.float32)
    tile_row = slots // tile_cols
    tile_col = slots % tile_cols
    row_select = (tile_row[:, None] == jnp.arange(tile_rows)[None, :]).astype(
        jnp.float32
    ) * live_mask[:, None]
    col_select = (tile_col[:, None] == jnp.arange(tile_cols)[None, :]).astype(
        jnp.float32
    ) * live_mask[:, None]
    dst_partial = jnp.dot(
        row_select.T, jnp.sum(adjacency, axis=2), precision=lax.Precision.HIGHEST
    ).reshape(-1)
    src_partial = jnp.dot(
        col_select.T, jnp.sum(adjacency, axis=1), precision=lax.Precision.HIGHEST
    ).reshape(-1)
    src_scale = lax.rsqrt(
        1.0 + lax.psum_scatter(src_partial, "row", scatter_dimension=0, tiled=True)
    )
    scaled = features * src_scale[:, None]
    gathered = lax.all_gather(scaled, "row", axis=0, tiled=True)
    taken = jnp.take(gathered.reshape(tile_cols, TILE, width), tile_col, axis=0)
    product = jnp.einsum(
        "kab,kbh->kah",
        adjacency,
        taken,
        precision=lax.Precision.HIGHEST,
        preferred_element_type=jnp.float32,
    )
    partial_value = jnp.einsum(
        "kr,kah->rah",
        row_select,
        product,
        precision=lax.Precision.HIGHEST,
        preferred_element_type=jnp.float32,
    ).reshape(tile_rows * TILE, width)
    dst_scale = lax.rsqrt(
        1.0 + lax.psum_scatter(dst_partial, "col", scatter_dimension=0, tiled=True)
    )
    aggregated = (
        lax.psum_scatter(partial_value, "col", scatter_dimension=0, tiled=True) * dst_scale[:, None]
    )
    activated, weight_part, bias_part, back_rows = dense_step(
        aggregated, weight, bias_vector, out_grad
    )
    weight_grad, bias_grad = lax.psum((weight_part, bias_part), ("row", "col"))
    row_grads = lax.all_gather(back_rows * dst_scale[:, None], "col", axis=0, tiled=True)
    taken_back = jnp.take(row_grads.reshape(tile_rows, TILE, width), tile_row, axis=0)
    product_back = jnp.einsum(
        "kab,kah->kbh",
        adjacency,
        taken_back,
        precision=lax.Precision.HIGHEST,
        preferred_element_type=jnp.float32,
    )
    partial_back = jnp.einsum(
        "kc,kbh->cbh",
        col_select,
        product_back,
        precision=lax.Precision.HIGHEST,
        preferred_element_type=jnp.float32,
    ).reshape(tile_cols * TILE, width)
    feature_grad = (
        lax.psum_scatter(partial_back, "row", scatter_dimension=0, tiled=True) * src_scale[:, None]
    )
    return (activated, feature_grad, weight_grad, bias_grad)


def solution(mesh):
    return jax.shard_map(
        local,
        mesh=mesh,
        in_specs=(
            P(("col", "row"), None),
            P(),
            P(),
            P(("row", "col"), None),
            P("row", "col", None, None, None),
            P("row", "col", None),
            P("row", "col"),
        ),
        out_specs=(P(("row", "col"), None), P(("col", "row"), None), P(), P()),
        check_vma=False,
    )
```

profile of v0, /device:TPU:1, one launch (start us, length us, event | category | flops | bytes accessed | tf_op | source)
XLA Modules:
  0.0 764.2 jit_solution(688655162839533169)
XLA Ops:
  7.2 0.0 copy-start
  7.2 0.0 copy-start.3
  7.2 0.0 copy-start.1
  7.2 0.0 all-gather.3.cloned.1.call-start
  7.9 1.3 dynamic-slice
  9.9 5.7 convert_reduce_fusion
  15.6 0.0 copy-done.3
  15.6 0.2 convolution_bitcast_fusion.1
  15.8 68.3 %all-reduce = f32[4096]{0:T(1024)S(1)} all-reduce(f32[4096]{0:T(1024)S(1)} %convolution_bitcast_fusion.1), channel_id=2, replica_groups=mesh['row'=16,'col'=16] {'row'}, use_global_device_ids=true, to_apply=%region_1.2.clone | all-reduce | flops 4096 | bytes 32768
  84.1 0.1 fusion.45
  84.2 0.0 copy-done.1
  84.2 0.8 broadcast_multiply_fusion.1
  85.0 0.0 all-gather.3.cloned.1.call-update
  85.0 0.0 reduce-scatter.3.cloned.1.call-start
  85.1 89.2 %all-gather.3.cloned.1.call-done = f32[4096,128]{1,0:T(8,128)} async-done(((f32[256,128]{1,0:T(8,128)}), f32[4096,128]{1,0:T(8,128)}) %all-gather.3.cloned.1.call-update) | async-done | bytes 2097168 | tf_op jit(solution)/shard_map/all_gather | solution.py:49
  174.3 5.9 gather_fusion
  180.1 21.5 %fusion.12 = f32[128,128,128]{1,2,0:T(8,128)} fusion(s32[1,1,128,128,128]{4,3,2,1,0:T(8,128)} %param.13, f32[128,128,128]{2,1,0:T(8,128)} %gather_fusion, pred[128]{0:T(512)(128)(4,1)S(1)} %get-tuple-element.14), kind=kOutput, calls=%fused_computation.16 | convolution fusion | flops 3225419776 | bytes 25165952 | tf_op jit(solution)/shard_map/kab,kbh->kah/dot_general | solution.py:51
  201.7 9.3 %copy.18 = f32[128,128,128]{2,0,1:T(8,128)} copy(f32[128,128,128]{1,2,0:T(8,128)} %fusion.12) | data formatting | bytes 16777216 | tf_op jit(solution)/shard_map/kab,kbh->kah/dot_general | solution.py:51
  211.0 0.0 copy-start.6
  211.0 0.0 copy-start.4
  211.0 0.0 copy-start.5
  211.0 6.8 fusion.30
  217.7 2.6 copy.19
  220.3 0.0 reduce-scatter.3.cloned.1.call-update
  220.3 0.0 all-gather.5.cloned.1.call-start
  220.4 0.0 copy-done.6
  220.4 0.6 dynamic-slice.2
  221.6 0.2 convolution_bitcast_fusion
  221.8 87.6 %all-reduce.1 = f32[4096]{0:T(1024)S(1)} all-reduce(f32[4096]{0:T(1024)S(1)} %convolution_bitcast_fusion), channel_id=4, replica_groups=mesh['row'=16,'col'=16] {'col'}, use_global_device_ids=true, to_apply=%region_4.6.clone | all-reduce | flops 4096 | bytes 32768
  309.4 0.1 fusion.44
  309.5 4.8 reduce-scatter.3.cloned.1.call-done
  314.3 0.0 copy-done
  314.3 0.0 copy-done.4
  314.3 0.0 copy-done.5
  314.3 1.9 fusion.52
  316.2 0.9 convolution_multiply_fusion
  317.1 0.0 all-gather.5.cloned.1.call-update
  317.2 0.0 reduce-scatter.5.cloned.1.call-start
  317.2 62.5 %all-gather.5.cloned.1.call-done = f32[4096,128]{1,0:T(8,128)} async-done(((f32[256,128]{1,0:T(8,128)}), f32[4096,128]{1,0:T(8,128)}) %all-gather.5.cloned.1.call-update) | async-done | bytes 2097168 | tf_op jit(solution)/shard_map/all_gather | solution.py:75
  379.7 5.9 gather_fusion.1
  385.6 19.7 %fusion.17 = f32[128,128,128]{1,2,0:T(8,128)} fusion(s32[1,1,128,128,128]{4,3,2,1,0:T(8,128)} %param.13, f32[128,128,128]{2,1,0:T(8,128)} %gather_fusion.1, pred[128]{0:T(512)(128)(4,1)S(1)} %get-tuple-element.9), kind=kOutput, calls=%fused_computation.17 | convolution fusion | flops 3225419776 | bytes 25165952 | tf_op jit(solution)/shard_map/kab,kah->kbh/dot_general | solution.py:77
  405.3 9.3 %copy.21 = f32[128,128,128]{2,0,1:T(8,128)} copy(f32[128,128,128]{1,2,0:T(8,128)} %fusion.17) | data formatting | bytes 16777216 | tf_op jit(solution)/shard_map/kab,kah->kbh/dot_general | solution.py:77
  414.6 0.0 copy-start.2
  414.6 6.8 fusion.31
  421.4 2.6 copy.22
  424.0 0.0 reduce-scatter.5.cloned.1.call-update
  424.0 0.0 all-reduce.4.cloned.1.call-start
  424.0 76.6 %psum.15 = f32[128]{0:T(128)} all-reduce(f32[128]{0:T(128)S(1)} %get-tuple-element.7), channel_id=1, replica_groups=mesh['row'=16,'col'=16] {'row','col'}, use_global_device_ids=true, to_apply=%region_8.10 | all-reduce | flops 128 | bytes 1024 | tf_op jit(solution)/shard_map/psum | solution.py:74
  500.6 0.0 copy-done.2
  500.6 1.1 fusion.23
  501.7 0.0 all-reduce.4.cloned.1.call-update
  501.7 0.0 reduce-scatter.5.cloned.1.call-done
  501.8 1.7 broadcast_multiply_fusion
  503.4 252.8 %all-reduce.4.cloned.1.call-done = f32[128,128]{1,0:T(8,128)} async-done(((f32[128,128]{1,0:T(8,128)}), f32[128,128]{1,0:T(8,128)}) %all-reduce.4.cloned.1.call-update) | async-done | bytes 65552 | tf_op jit(solution)/shard_map/psum | solution.py:74
  756.2 1.5 copy.27
  (5 shorter events, 0.0 us)
Async XLA Ops:
  7.2 307.1 %copy-start = (f32[128,128]{1,0:T(8,128)S(1)}, f32[128,128]{1,0:T(8,128)}, u32[]{:S(2)}) copy-start(f32[128,128]{1,0:T(8,128)} %param.10) | copy-start | bytes 196612
  7.2 8.4 %copy-start.3 = (s32[1,1,128]{2,1,0:T(1,128)S(1)}, s32[1,1,128]{2,1,0:T(1,128)}, u32[]{:S(2)}) copy-start(s32[1,1,128]{2,1,0:T(1,128)} %param.14) | copy-start | bytes 1540
  7.2 77.0 %copy-start.1 = (f32[256,128]{1,0:T(8,128)S(1)}, f32[256,128]{1,0:T(8,128)}, u32[]{:S(2)}) copy-start(f32[256,128]{1,0:T(8,128)} %param.9) | copy-start | bytes 393220
  7.2 167.1 %all-gather.3.cloned.1.call-start = ((), (), s32[]{:S(2)}) async-start(), calls=%async_computation.2 | async-start | bytes 2228224 | tf_op jit(solution)/shard_map/all_gather | solution.py:49
  85.0 229.3 %reduce-scatter.3.cloned.1.call-start = ((), (), s32[]{:S(2)}) async-start(), calls=%async_computation.3 | async-start | bytes 2228224 | tf_op jit(solution)/shard_map/reduce_scatter | solution.py:69
  211.0 9.4 %copy-start.6 = (u32[256]{0:T(256)S(1)}, u32[256]{0:T(256)}, u32[]{:S(2)}) copy-start(u32[256]{0:T(256)} %constant.56) | copy-start | bytes 3076
  211.0 103.3 %copy-start.4 = (f32[256,128]{1,0:T(8,128)S(1)}, f32[256,128]{1,0:T(8,128)}, u32[]{:S(2)}) copy-start(f32[256,128]{1,0:T(8,128)} %param.12) | copy-start | bytes 393220
  211.0 103.3 %copy-start.5 = (f32[128]{0:T(128)S(1)}, f32[128]{0:T(128)}, u32[]{:S(2)}) copy-start(f32[128]{0:T(128)} %param.11) | copy-start | bytes 1540
  220.3 159.4 %all-gather.5.cloned.1.call-start = ((), (), s32[]{:S(2)}) async-start(), calls=%async_computation.4 | async-start | bytes 2228224 | tf_op jit(solution)/shard_map/all_gather | solution.py:75
  317.2 184.6 %reduce-scatter.5.cloned.1.call-start = ((), (), s32[]{:S(2)}) async-start(), calls=%async_computation.5 | async-start | bytes 2228224 | tf_op jit(solution)/shard_map/reduce_scatter | solution.py:92
  414.6 86.0 %copy-start.2 = (f32[256,128]{1,0:T(8,128)S(1)}, f32[256,128]{1,0:T(8,128)}, u32[]{:S(2)}) copy-start(f32[256,128]{1,0:T(8,128)} %reduce-scatter.3.cloned.1.call-done) | copy-start | bytes 393220
  424.0 332.2 %all-reduce.4.cloned.1.call-start = ((), (), s32[]{:S(2)}) async-start(), calls=%async_computation.6 | async-start | bytes 131072 | tf_op jit(solution)/shard_map/psum | solution.py:74
Sparse Core Ops, SparseCore 0:
  85.1 89.0 all-gather.2
  220.5 93.7 reduce-scatter.2
  317.5 62.1 all-gather.4
  424.1 77.1 reduce-scatter.4
  507.3 248.8 all-reduce.3
where the time goes:
time: 765 us; the launch traced here: 764 us
  waiting for transfers between devices  409 us (53%)
  blocking collectives  232 us (30%)
  matrix products  59 us (8%)
  local copies, waits for them, and re-layouts  38.9 us (5%)
  between operations  15.9 us (2%)
  other arithmetic  8.34 us (1%)
    psum x1, waiting for transfers between devices, local(): weight_grad, bias_grad = lax.psum((weight_part, bias_part), ('row', 'col'))  253 us
    unnamed x2, blocking collectives  156 us
    all_gather x1, waiting for transfers between devices, local(): gathered = lax.all_gather(scaled, 'row', axis=0, tiled=True)  89.2 us
    psum x1, blocking collectives, local(): weight_grad, bias_grad = lax.psum((weight_part, bias_part), ('row', 'col'))  76.6 us
    all_gather x1, waiting for transfers between devices, local(): lax.all_gather(back_rows * dst_scale[:, None], 'col', axis=0, tiled=True)  62.5 us
    dot_general x1, matrix products, local(): jnp.einsum('kab,kbh->kah', adjacency, taken, precision=lax.Precision.HIGH...  21.5 us
    dot_general x1, matrix products, local(): jnp.einsum('kab,kah->kbh', adjacency, taken_back, precision=lax.Precision...  19.7 us
  transfers between devices with their start and end apart: 5, of which 4 were waited for; matrix products, arithmetic and copies ran while one was open for 0% of the time, Pallas kernels for 0%

commit v1 on v0

--- a/solution.py
+++ b/solution.py
@@ -4,6 +4,11 @@
 from jax.sharding import PartitionSpec as P
 
 TILE = 128
+
+
+def axis_by_axis(array, inner_axis, outer_axis):
+    partial = lax.psum(array, inner_axis)
+    return lax.psum(partial, outer_axis)
 
 
 def dense_step(aggregated, weight, bias_vector, cotangent):
@@ -71,7 +76,7 @@
     activated, weight_part, bias_part, back_rows = dense_step(
         aggregated, weight, bias_vector, out_grad
     )
-    weight_grad, bias_grad = lax.psum((weight_part, bias_part), ("row", "col"))
+    weight_grad, bias_grad = axis_by_axis((weight_part, bias_part), "col", "row")
     row_grads = lax.all_gather(back_rows * dst_scale[:, None], "col", axis=0, tiled=True)
     taken_back = jnp.take(row_grads.reshape(tile_rows, TILE, width), tile_row, axis=0)
     product_back = jnp.einsum(

time: 765 us -> 795 us (1.039); the launches traced: 764 us -> 786 us
  waiting for transfers between devices: 409 us -> 430 us
    reduce_scatter x1, waiting for transfers between devices: 0.02 us -> 84 us  [local(): lax.psum_scatter(partial_back, 'row', scatter_dimension=0, tiled=True)]
    psum x1 -> x2, waiting for transfers between devices: 253 us -> 192 us  [the longest x1 148 us: axis_by_axis(): return lax.psum(partial, outer_axis)]
    psum x1 -> x2, blocking collectives: 76.6 us -> 76 us  [the longest x1 42.4 us: axis_by_axis(): partial = lax.psum(array, inner_axis)]
  transfers between devices with their start and end apart: 5 -> 6, of which waited for: 4 -> 6; matrix products, arithmetic and copies ran while one was open for 0% -> 6% of each run, Pallas kernels for 0% -> 0%
where the time goes in v1:
time: 795 us; the launch traced here: 786 us
  waiting for transfers between devices  430 us (54%)
  blocking collectives  232 us (29%)
  matrix products  59.9 us (8%)
  local copies, waits for them, and re-layouts  38.9 us (5%)
  between operations  16.2 us (2%)
  other arithmetic  8.34 us (1%)
    unnamed x2, blocking collectives  156 us
    psum x1, waiting for transfers between devices, axis_by_axis(): return lax.psum(partial, outer_axis)  148 us
    all_gather x1, waiting for transfers between devices, local(): gathered = lax.all_gather(scaled, 'row', axis=0, tiled=True)  89.2 us
    reduce_scatter x1, waiting for transfers between devices, local(): lax.psum_scatter(partial_back, 'row', scatter_dimension=0, tiled=True)  84 us
    all_gather x1, waiting for transfers between devices, local(): lax.all_gather(back_rows * dst_scale[:, None], 'col', axis=0, tiled=True)  60 us
    psum x1, waiting for transfers between devices, axis_by_axis(): partial = lax.psum(array, inner_axis)  44 us
    psum x1, blocking collectives, axis_by_axis(): partial = lax.psum(array, inner_axis)  42.4 us
    psum x1, blocking collectives, axis_by_axis(): return lax.psum(partial, outer_axis)  33.6 us
  transfers between devices with their start and end apart: 6, of which 6 were waited for; matrix products, arithmetic and copies ran while one was open for 6% of the time, Pallas kernels for 0%

profile of v1, /device:TPU:1, one launch (start us, length us, event | category | flops | bytes accessed | tf_op | source)
XLA Modules:
  0.0 785.9 jit_solution(5417639628907981225)
XLA Ops:
  7.2 0.0 copy-start
  7.2 0.0 copy-start.2
  7.2 0.0 copy-start.1
  7.2 0.0 all-gather.3.cloned.1.call-start
  7.9 1.3 dynamic-slice
  9.9 5.7 convert_reduce_fusion
  15.6 0.0 copy-done.2
  15.6 0.2 convolution_bitcast_fusion.1
  15.8 68.3 %all-reduce = f32[4096]{0:T(1024)S(1)} all-reduce(f32[4096]{0:T(1024)S(1)} %convolution_bitcast_fusion.1), channel_id=2, replica_groups=mesh['row'=16,'col'=16] {'row'}, use_global_device_ids=true, to_apply=%region_1.2.clone | all-reduce | flops 4096 | bytes 32768
  84.1 0.1 fusion.45
  84.2 0.0 copy-done.1
  84.2 0.8 broadcast_multiply_fusion.1
  85.0 0.0 all-gather.3.cloned.1.call-update
  85.0 0.0 reduce-scatter.3.cloned.1.call-start
  85.1 89.2 %all-gather.3.cloned.1.call-done = f32[4096,128]{1,0:T(8,128)} async-done(((f32[256,128]{1,0:T(8,128)}), f32[4096,128]{1,0:T(8,128)}) %all-gather.3.cloned.1.call-update) | async-done | bytes 2097168 | tf_op jit(solution)/shard_map/all_gather | solution.py:54
  174.3 5.9 gather_fusion
  180.1 21.5 %fusion.12 = f32[128,128,128]{1,2,0:T(8,128)} fusion(s32[1,1,128,128,128]{4,3,2,1,0:T(8,128)} %param.13, f32[128,128,128]{2,1,0:T(8,128)} %gather_fusion, pred[128]{0:T(512)(128)(4,1)S(1)} %get-tuple-element.14), kind=kOutput, calls=%fused_computation.16 | convolution fusion | flops 3225419776 | bytes 25165952 | tf_op jit(solution)/shard_map/kab,kbh->kah/dot_general | solution.py:56
  201.7 9.3 %copy.18 = f32[128,128,128]{2,0,1:T(8,128)} copy(f32[128,128,128]{1,2,0:T(8,128)} %fusion.12) | data formatting | bytes 16777216 | tf_op jit(solution)/shard_map/kab,kbh->kah/dot_general | solution.py:56
  211.0 0.0 copy-start.5
  211.0 0.0 copy-start.3
  211.0 0.0 copy-start.4
  211.0 6.8 fusion.30
  217.8 2.6 copy.19
  220.3 0.0 reduce-scatter.3.cloned.1.call-update
  220.3 0.0 all-gather.5.cloned.1.call-start
  220.4 0.0 copy-done.5
  220.4 0.6 dynamic-slice.2
  221.6 0.2 convolution_bitcast_fusion
  221.8 87.6 %all-reduce.1 = f32[4096]{0:T(1024)S(1)} all-reduce(f32[4096]{0:T(1024)S(1)} %convolution_bitcast_fusion), channel_id=4, replica_groups=mesh['row'=16,'col'=16] {'col'}, use_global_device_ids=true, to_apply=%region_4.6.clone | all-reduce | flops 4096 | bytes 32768
  309.4 0.1 fusion.44
  309.5 5.2 reduce-scatter.3.cloned.1.call-done
  314.7 0.0 copy-done
  314.7 0.0 copy-done.3
  314.7 0.0 copy-done.4
  314.7 1.9 fusion.52
  316.7 0.9 convolution_multiply_fusion
  317.6 0.0 all-gather.5.cloned.1.call-update
  317.6 0.0 all-reduce.5.cloned.1.call-start
  317.7 2.0 fusion.23
  319.7 0.0 all-reduce.5.cloned.1.call-update
  319.7 0.0 reduce-scatter.5.cloned.1.call-start
  319.8 60.0 %all-gather.5.cloned.1.call-done = f32[4096,128]{1,0:T(8,128)} async-done(((f32[256,128]{1,0:T(8,128)}), f32[4096,128]{1,0:T(8,128)}) %all-gather.5.cloned.1.call-update) | async-done | bytes 2097168 | tf_op jit(solution)/shard_map/all_gather | solution.py:80
  379.7 5.9 gather_fusion.1
  385.6 19.7 %fusion.17 = f32[128,128,128]{1,2,0:T(8,128)} fusion(s32[1,1,128,128,128]{4,3,2,1,0:T(8,128)} %param.13, f32[128,128,128]{2,1,0:T(8,128)} %gather_fusion.1, pred[128]{0:T(512)(128)(4,1)S(1)} %get-tuple-element.9), kind=kOutput, calls=%fused_computation.17 | convolution fusion | flops 3225419776 | bytes 25165952 | tf_op jit(solution)/shard_map/kab,kah->kbh/dot_general | solution.py:82
  405.4 9.3 %copy.21 = f32[128,128,128]{2,0,1:T(8,128)} copy(f32[128,128,128]{1,2,0:T(8,128)} %fusion.17) | data formatting | bytes 16777216 | tf_op jit(solution)/shard_map/kab,kah->kbh/dot_general | solution.py:82
  414.7 6.7 fusion.31
  421.4 2.6 copy.22
  424.0 0.0 reduce-scatter.5.cloned.1.call-update
  424.0 0.0 all-reduce.7.cloned.1.call-start
  424.0 42.4 %psum.30 = f32[128]{0:T(128)S(1)} all-reduce(f32[128]{0:T(128)S(1)} %get-tuple-element.7), channel_id=1, replica_groups=mesh['row'=16,'col'=16] {'col'}, use_global_device_ids=true, to_apply=%region_9.11 | all-reduce | flops 128 | bytes 1024 | tf_op jit(solution)/shard_map/psum | solution.py:10
  466.5 33.6 %psum.31 = f32[128]{0:T(128)} all-reduce(f32[128]{0:T(128)S(1)} %psum.30), channel_id=1, replica_groups=mesh['row'=16,'col'=16] {'row'}, use_global_device_ids=true, to_apply=%region_10.12 | all-reduce | flops 128 | bytes 1024 | tf_op jit(solution)/shard_map/psum | solution.py:11
  500.0 44.0 %all-reduce.5.cloned.1.call-done = f32[128,128]{1,0:T(8,128)} async-done(((f32[128,128]{1,0:T(8,128)}), f32[128,128]{1,0:T(8,128)}) %all-reduce.5.cloned.1.call-update) | async-done | bytes 65552 | tf_op jit(solution)/shard_map/psum | solution.py:10
  544.1 0.0 all-reduce.7.cloned.1.call-update
  544.1 84.0 %reduce-scatter.5.cloned.1.call-done = f32[256,128]{1,0:T(8,128)} async-done(((f32[4096,128]{1,0:T(8,128)}), f32[256,128]{1,0:T(8,128)}) %reduce-scatter.5.cloned.1.call-update) | async-done | bytes 131088 | tf_op jit(solution)/shard_map/reduce_scatter | solution.py:97
  628.1 1.7 broadcast_multiply_fusion
  629.8 147.8 %all-reduce.7.cloned.1.call-done = f32[128,128]{1,0:T(8,128)} async-done(((f32[128,128]{1,0:T(8,128)}), f32[128,128]{1,0:T(8,128)}) %all-reduce.7.cloned.1.call-update) | async-done | bytes 65552 | tf_op jit(solution)/shard_map/psum | solution.py:11
  777.6 1.5 copy.28
  (5 shorter events, 0.0 us)
Async XLA Ops:
  7.2 307.6 %copy-start = (f32[128,128]{1,0:T(8,128)S(1)}, f32[128,128]{1,0:T(8,128)}, u32[]{:S(2)}) copy-start(f32[128,128]{1,0:T(8,128)} %param.10) | copy-start | bytes 196612
  7.2 8.4 %copy-start.2 = (s32[1,1,128]{2,1,0:T(1,128)S(1)}, s32[1,1,128]{2,1,0:T(1,128)}, u32[]{:S(2)}) copy-start(s32[1,1,128]{2,1,0:T(1,128)} %param.14) | copy-start | bytes 1540
  7.2 77.0 %copy-start.1 = (f32[256,128]{1,0:T(8,128)S(1)}, f32[256,128]{1,0:T(8,128)}, u32[]{:S(2)}) copy-start(f32[256,128]{1,0:T(8,128)} %param.9) | copy-start | bytes 393220
  7.2 167.1 %all-gather.3.cloned.1.call-start = ((), (), s32[]{:S(2)}) async-start(), calls=%async_computation.2 | async-start | bytes 2228224 | tf_op jit(solution)/shard_map/all_gather | solution.py:54
  85.0 229.7 %reduce-scatter.3.cloned.1.call-start = ((), (), s32[]{:S(2)}) async-start(), calls=%async_computation.3 | async-start | bytes 2228224 | tf_op jit(solution)/shard_map/reduce_scatter | solution.py:74
  211.0 9.4 %copy-start.5 = (u32[256]{0:T(256)S(1)}, u32[256]{0:T(256)}, u32[]{:S(2)}) copy-start(u32[256]{0:T(256)} %constant.56) | copy-start | bytes 3076
  211.0 103.7 %copy-start.3 = (f32[256,128]{1,0:T(8,128)S(1)}, f32[256,128]{1,0:T(8,128)}, u32[]{:S(2)}) copy-start(f32[256,128]{1,0:T(8,128)} %param.12) | copy-start | bytes 393220
  211.0 103.7 %copy-start.4 = (f32[128]{0:T(128)S(1)}, f32[128]{0:T(128)}, u32[]{:S(2)}) copy-start(f32[128]{0:T(128)} %param.11) | copy-start | bytes 1540
  220.3 159.4 %all-gather.5.cloned.1.call-start = ((), (), s32[]{:S(2)}) async-start(), calls=%async_computation.4 | async-start | bytes 2228224 | tf_op jit(solution)/shard_map/all_gather | solution.py:80
  317.6 226.5 %all-reduce.5.cloned.1.call-start = ((), (), s32[]{:S(2)}) async-start(), calls=%async_computation.6 | async-start | bytes 131072 | tf_op jit(solution)/shard_map/psum | solution.py:10
  319.7 308.4 %reduce-scatter.5.cloned.1.call-start = ((), (), s32[]{:S(2)}) async-start(), calls=%async_computation.5 | async-start | bytes 2228224 | tf_op jit(solution)/shard_map/reduce_scatter | solution.py:97
  424.0 353.6 %all-reduce.7.cloned.1.call-start = ((), (), s32[]{:S(2)}) async-start(), calls=%async_computation.7 | async-start | bytes 131072 | tf_op jit(solution)/shard_map/psum | solution.py:11
Sparse Core Ops, SparseCore 0:
  85.1 89.0 all-gather.2
  220.5 94.2 reduce-scatter.2
  318.0 61.7 all-gather.4
  382.8 161.2 all-reduce.4
  546.5 81.5 reduce-scatter.4
  630.6 146.9 all-reduce.6
